TPU v7x, 32 devices: a whole 2x2x4 slice. The times are simulated.
32 devices in a mesh: fsdp: 8 (over z, y), tp: 4 (over x, core).
Axes of the slice: x: 2, y: 2, z: 4, core: 2. Of those that a mesh axis runs over, the one named last changes fastest.
Arguments:
- inputs: bfloat16 [16, 736, 1152], P('fsdp', 'tp'), may hold values from -6 to 6
- cotangent: bfloat16 [16, 736, 1152], P('fsdp', 'tp'), may hold values from -6 to 6
- lengths: int32 [16], P('fsdp'), may hold values from 1 to 729, as said below
- ln1_gain: bfloat16 [1152], P('fsdp'), may hold values from 0.099609375 to 1.8984375
- ln1_bias: bfloat16 [1152], P('fsdp'), may hold values from -0.3125 to 0.3125
- q_weight: bfloat16 [1152, 1152], P('fsdp', 'tp'), may hold values from -0.1875 to 0.1875
- q_bias: bfloat16 [1152], P('tp'), may hold values from -3 to 3
- k_weight: bfloat16 [1152, 1152], P('fsdp', 'tp'), may hold values from -0.1875 to 0.1875
- v_weight: bfloat16 [1152, 1152], P('fsdp', 'tp'), may hold values from -0.1875 to 0.1875
- v_bias: bfloat16 [1152], P('tp'), may hold values from -0.1875 to 0.1875
- out_weight: bfloat16 [1152, 1152], P('tp', 'fsdp'), may hold values from -2.5 to 2.5
- out_bias: bfloat16 [1152], P('fsdp'), may hold values from -1.75 to 1.75
- ln2_gain: bfloat16 [1152], P('fsdp'), may hold values from 0.099609375 to 1.8984375
- ln2_bias: bfloat16 [1152], P('fsdp'), may hold values from -1.75 to 1.75
- up_weight: bfloat16 [1152, 4304], P('fsdp', 'tp'), may hold values from -0.1875 to 0.1875
- up_bias: bfloat16 [4304], P('tp'), may hold values from -1.75 to 1.75
- down_weight: bfloat16 [4304, 1152], P('tp', 'fsdp'), may hold values from -0.09375 to 0.09375
- down_bias: bfloat16 [1152], P('fsdp'), may hold values from -1.75 to 1.75
Outputs:
- layer_out: bfloat16 [16, 736, 1152], P('fsdp', 'tp')
- input_grad: float32 [16, 736, 1152], P('fsdp', 'tp')
- ln1_gain_grad: float32 [1152], P('fsdp')
- ln1_bias_grad: float32 [1152], P('fsdp')
- q_weight_grad: float32 [1152, 1152], P('fsdp', 'tp')
- q_bias_grad: float32 [1152], P('tp')
- k_weight_grad: float32 [1152, 1152], P('fsdp', 'tp')
- v_weight_grad: float32 [1152, 1152], P('fsdp', 'tp')
- v_bias_grad: float32 [1152], P('tp')
- out_weight_grad: float32 [1152, 1152], P('tp', 'fsdp')
- out_bias_grad: float32 [1152], P('fsdp')
- ln2_gain_grad: float32 [1152], P('fsdp')
- ln2_bias_grad: float32 [1152], P('fsdp')
- up_weight_grad: float32 [1152, 4304], P('fsdp', 'tp')
- up_bias_grad: float32 [4304], P('tp')
- down_weight_grad: float32 [4304, 1152], P('tp', 'fsdp')
- down_bias_grad: float32 [1152], P('fsdp')
Inputs may be any that keep to these rules, and one draw needn't show every extreme that they name: `lengths`: each slot either holds one image of 729 tokens or is empty with length 1; exactly 11 slots hold images, which ones drawn from the seed.
All inputs are finite; a program needn't handle non-finite values.
Results may differ from a plain program's by a relative error of at most 0.013.
Values may be sent and summed in bfloat16 or wider, within the bound.
No kernel may reach another device: no remote copies, remote signals or barrier semaphores. Data moves between devices by JAX's collectives and lax.ppermute only.
A program may use at most 192 MiB of HBM per device.

v0:
```python
import jax
import jax.numpy as jnp
from jax import lax
from jax.sharding import PartitionSpec as P

HD = 72
epsilon = 1e-06
negative_big = -1e30


def layer_norm(row_block, gain_vec, shift_vec):
    average = jnp.mean(row_block, -1, keepdims=True)
    center = row_block - average
    variance = jnp.mean(center * center, -1, keepdims=True)
    return center * lax.rsqrt(variance + epsilon) * gain_vec + shift_vec


def gelu_tanh(values_in):
    return jax.nn.gelu(values_in, approximate=True)


def plain_dot(left, right):
    return jnp.dot(left, right, preferred_element_type=jnp.float32)


def contract_rows(left, right):
    return lax.dot_general(
        left, right, (((0,), (0,)), ((), ())), preferred_element_type=jnp.float32
    )


def contract_cols(left, right):
    return lax.dot_general(
        left, right, (((1,), (1,)), ((), ())), preferred_element_type=jnp.float32
    )


def local(
    inputs,
    cotangent,
    lengths,
    ln1_gain,
    ln1_bias,
    q_weight,
    q_bias,
    k_weight,
    v_weight,
    v_bias,
    out_weight,
    out_bias,
    ln2_gain,
    ln2_bias,
    up_weight,
    up_bias,
    down_weight,
    down_bias,
):
    tp_count = lax.axis_size("tp")
    tp_index = lax.axis_index("tp")
    fsdp_index = lax.axis_index("fsdp")
    micro_count = inputs.shape[0]
    local_rows = inputs.shape[1]
    model_width = inputs.shape[2]
    seq_len = local_rows * tp_count
    head_width = q_weight.shape[1]
    heads_here = head_width // HD
    unit_width = up_weight.shape[1]
    scale_value = HD ** (-0.5)
    q_shift = q_bias.astype(jnp.float32)
    v_shift = v_bias.astype(jnp.float32)
    up_shift = up_bias.astype(jnp.float32)

    def fetch_weights():
        attn_full = (
            lax.all_gather(ln1_gain, "fsdp", axis=0, tiled=True),
            lax.all_gather(ln1_bias, "fsdp", axis=0, tiled=True),
            lax.all_gather(q_weight, "fsdp", axis=0, tiled=True),
            lax.all_gather(k_weight, "fsdp", axis=0, tiled=True),
            lax.all_gather(v_weight, "fsdp", axis=0, tiled=True),
            lax.all_gather(out_weight, "fsdp", axis=1, tiled=True),
            lax.all_gather(out_bias, "fsdp", axis=0, tiled=True),
        )
        mlp_full = (
            lax.all_gather(ln2_gain, "fsdp", axis=0, tiled=True),
            lax.all_gather(ln2_bias, "fsdp", axis=0, tiled=True),
            lax.all_gather(up_weight, "fsdp", axis=0, tiled=True),
            lax.all_gather(down_weight, "fsdp", axis=1, tiled=True),
            lax.all_gather(down_bias, "fsdp", axis=0, tiled=True),
        )
        return (attn_full, mlp_full)

    def masked_scores(queries, keys_all, key_valid):
        query_heads = queries.reshape(seq_len, heads_here, HD)
        key_heads = keys_all.reshape(seq_len, heads_here, HD)
        scores = (
            jnp.einsum("qhd,khd->hqk", query_heads, key_heads, preferred_element_type=jnp.float32)
            * scale_value
        )
        return jnp.where(key_valid[None, None, :], scores, negative_big)

    def forward(slot_rows, length, attn_full, mlp_full):
        gain_one, shift_one, wq_full, wk_full, wv_full, wo_full, bo_full = attn_full
        gain_two, shift_two, w_up, w_down, bd_full = mlp_full
        key_valid = jnp.arange(seq_len, dtype=jnp.int32) < length
        norm_one = layer_norm(
            slot_rows, gain_one.astype(jnp.float32), shift_one.astype(jnp.float32)
        ).astype(jnp.bfloat16)
        norm_full = lax.all_gather(norm_one, "tp", axis=0, tiled=True)
        queries = (plain_dot(norm_full, wq_full) + q_shift).astype(jnp.bfloat16)
        keys_all = plain_dot(norm_full, wk_full).astype(jnp.bfloat16)
        values_all = (plain_dot(norm_full, wv_full) + v_shift).astype(jnp.bfloat16)
        scores = masked_scores(queries, keys_all, key_valid)
        row_max = jnp.max(scores, -1, keepdims=True)
        row_total = jnp.sum(jnp.exp(scores - row_max), -1, keepdims=True)
        log_total = row_max + jnp.log(row_total)
        soft_low = jnp.exp(scores - log_total).astype(jnp.bfloat16)
        value_heads = values_all.reshape(seq_len, heads_here, HD)
        mixed_heads = jnp.einsum(
            "hqk,khd->qhd", soft_low, value_heads, preferred_element_type=jnp.float32
        )
        mixed_heads = mixed_heads.astype(jnp.bfloat16).reshape(seq_len, head_width)
        attended = lax.psum_scatter(
            plain_dot(mixed_heads, wo_full), "tp", scatter_dimension=0, tiled=True
        )
        middle = slot_rows + attended + bo_full.astype(jnp.float32)
        norm_two = layer_norm(
            middle, gain_two.astype(jnp.float32), shift_two.astype(jnp.float32)
        ).astype(jnp.bfloat16)
        norm_two_full = lax.all_gather(norm_two, "tp", axis=0, tiled=True)
        hidden = plain_dot(norm_two_full, w_up) + up_shift
        active = gelu_tanh(hidden).astype(jnp.bfloat16)
        mlp_rows = lax.psum_scatter(
            plain_dot(active, w_down), "tp", scatter_dimension=0, tiled=True
        )
        out_rows = middle + mlp_rows + bd_full.astype(jnp.float32)
        kept_state = (
            norm_full,
            queries,
            keys_all,
            values_all,
            log_total,
            mixed_heads,
            middle,
            norm_two_full,
            hidden,
            active,
        )
        return (out_rows, kept_state)

    outputs = []
    for slot_index in range(micro_count):
        attn_full, mlp_full = fetch_weights()
        out_rows, kept_state = forward(
            inputs[slot_index].astype(jnp.float32), lengths[slot_index], attn_full, mlp_full
        )
        outputs.append(out_rows.astype(jnp.bfloat16))
    grad_list = []
    totals = None
    for slot_index in range(micro_count):
        attn_full, mlp_full = fetch_weights()
        slot_rows = inputs[slot_index].astype(jnp.float32)
        kept_state = forward(slot_rows, lengths[slot_index], attn_full, mlp_full)[1]
        backward_length = lengths[slot_index]
        (
            backward_gain_one,
            backward_shift_one,
            backward_wq_full,
            backward_wk_full,
            backward_wv_full,
            backward_wo_full,
            backward_bo_full,
        ) = attn_full
        backward_gain_two, backward_shift_two, backward_w_up, backward_w_down, backward_bd_full = (
            mlp_full
        )
        (
            backward_norm_full,
            backward_queries,
            backward_keys_all,
            backward_values_all,
            backward_log_total,
            backward_mixed_heads,
            backward_middle,
            backward_norm_two_full,
            backward_hidden,
            backward_active,
        ) = kept_state
        backward_key_valid = jnp.arange(seq_len, dtype=jnp.int32) < backward_length
        row_valid = (
            jnp.arange(local_rows, dtype=jnp.int32) + tp_index * local_rows < backward_length
        ).astype(jnp.float32)
        grad_out = cotangent[slot_index].astype(jnp.float32) * row_valid[:, None]
        backward_down_sum = jnp.sum(grad_out, 0)
        grad_out_full = lax.all_gather(grad_out.astype(jnp.bfloat16), "tp", axis=0, tiled=True)
        backward_grad_w_down = contract_rows(backward_active, grad_out_full)
        grad_active = contract_cols(grad_out_full, backward_w_down)
        gelu_pull = jax.vjp(gelu_tanh, backward_hidden)[1]
        grad_hidden = gelu_pull(grad_active)[0].astype(jnp.bfloat16)
        backward_up_sum = jnp.sum(grad_hidden.astype(jnp.float32), 0)
        backward_grad_w_up = contract_rows(backward_norm_two_full, grad_hidden)
        grad_norm_two = lax.psum_scatter(
            contract_cols(grad_hidden, backward_w_up), "tp", scatter_dimension=0, tiled=True
        )
        norm_two_pull = jax.vjp(
            layer_norm,
            backward_middle,
            backward_gain_two.astype(jnp.float32),
            backward_shift_two.astype(jnp.float32),
        )[1]
        middle_part, backward_gain_two_grad, backward_shift_two_grad = norm_two_pull(grad_norm_two)
        grad_middle = grad_out + middle_part
        backward_out_sum = jnp.sum(grad_middle, 0)
        grad_middle_full = lax.all_gather(
            grad_middle.astype(jnp.bfloat16), "tp", axis=0, tiled=True
        )
        backward_grad_w_out = contract_rows(backward_mixed_heads, grad_middle_full)
        grad_mixed = (
            contract_cols(grad_middle_full, backward_wo_full)
            .astype(jnp.bfloat16)
            .reshape(seq_len, heads_here, HD)
        )
        soft_weights = jnp.exp(
            masked_scores(backward_queries, backward_keys_all, backward_key_valid)
            - backward_log_total
        )
        backward_soft_low = soft_weights.astype(jnp.bfloat16)
        backward_query_heads = backward_queries.reshape(seq_len, heads_here, HD)
        backward_key_heads = backward_keys_all.reshape(seq_len, heads_here, HD)
        backward_value_heads = backward_values_all.reshape(seq_len, heads_here, HD)
        grad_soft = jnp.einsum(
            "qhd,khd->hqk", grad_mixed, backward_value_heads, preferred_element_type=jnp.float32
        )
        row_inner = jnp.sum(soft_weights * grad_soft, -1, keepdims=True)
        grad_scores = (soft_weights * (grad_soft - row_inner)).astype(jnp.bfloat16)
        grad_queries = (
            (
                jnp.einsum(
                    "hqk,khd->qhd",
                    grad_scores,
                    backward_key_heads,
                    preferred_element_type=jnp.float32,
                )
                * scale_value
            )
            .astype(jnp.bfloat16)
            .reshape(seq_len, head_width)
        )
        grad_keys = (
            (
                jnp.einsum(
                    "hqk,qhd->khd",
                    grad_scores,
                    backward_query_heads,
                    preferred_element_type=jnp.float32,
                )
                * scale_value
            )
            .astype(jnp.bfloat16)
            .reshape(seq_len, head_width)
        )
        grad_values = (
            jnp.einsum(
                "hqk,qhd->khd", backward_soft_low, grad_mixed, preferred_element_type=jnp.float32
            )
            .astype(jnp.bfloat16)
            .reshape(seq_len, head_width)
        )
        backward_query_sum = jnp.sum(grad_queries.astype(jnp.float32), 0)
        backward_value_sum = jnp.sum(grad_values.astype(jnp.float32), 0)
        backward_grad_wq = contract_rows(backward_norm_full, grad_queries)
        backward_grad_wk = contract_rows(backward_norm_full, grad_keys)
        backward_grad_wv = contract_rows(backward_norm_full, grad_values)
        part_q = contract_cols(grad_queries, backward_wq_full)
        part_k = contract_cols(grad_keys, backward_wk_full)
        part_v = contract_cols(grad_values, backward_wv_full)
        grad_norm_one = lax.psum_scatter(
            part_q + part_k + part_v, "tp", scatter_dimension=0, tiled=True
        )
        norm_one_pull = jax.vjp(
            layer_norm,
            slot_rows,
            backward_gain_one.astype(jnp.float32),
            backward_shift_one.astype(jnp.float32),
        )[1]
        rows_part, backward_gain_one_grad, backward_shift_one_grad = norm_one_pull(grad_norm_one)
        grad_rows = grad_middle + rows_part
        slot_grads = (
            backward_gain_one_grad,
            backward_shift_one_grad,
            backward_grad_wq,
            backward_query_sum,
            backward_grad_wk,
            backward_grad_wv,
            backward_value_sum,
            backward_grad_w_out,
            backward_out_sum,
            backward_gain_two_grad,
            backward_shift_two_grad,
            backward_grad_w_up,
            backward_up_sum,
            backward_grad_w_down,
            backward_down_sum,
        )
        grad_rows, slot_grads = (grad_rows, slot_grads)
        grad_list.append(grad_rows)
        if totals is None:
            totals = slot_grads
        else:
            totals = jax.tree.map(jnp.add, totals, slot_grads)
    (
        gain_one_grad,
        shift_one_grad,
        grad_wq,
        query_sum,
        grad_wk,
        grad_wv,
        value_sum,
        grad_w_out,
        out_sum,
        gain_two_grad,
        shift_two_grad,
        grad_w_up,
        up_sum,
        grad_w_down,
        down_sum,
    ) = totals
    summed_weights = (
        lax.psum_scatter(grad_wq, "fsdp", scatter_dimension=0, tiled=True),
        lax.psum_scatter(grad_wk, "fsdp", scatter_dimension=0, tiled=True),
        lax.psum_scatter(grad_wv, "fsdp", scatter_dimension=0, tiled=True),
        lax.psum_scatter(grad_w_out, "fsdp", scatter_dimension=1, tiled=True),
        lax.psum_scatter(grad_w_up, "fsdp", scatter_dimension=0, tiled=True),
        lax.psum_scatter(grad_w_down, "fsdp", scatter_dimension=1, tiled=True),
    )
    width_stack = jnp.stack(
        [gain_one_grad, shift_one_grad, out_sum, gain_two_grad, shift_two_grad, down_sum], 0
    )
    head_stack = jnp.zeros((2, head_width * tp_count), jnp.float32)
    head_stack = lax.dynamic_update_slice_in_dim(
        head_stack, jnp.stack([query_sum, value_sum], 0), tp_index * head_width, 1
    )
    unit_line = jnp.zeros((unit_width * tp_count,), jnp.float32)
    unit_line = lax.dynamic_update_slice_in_dim(unit_line, up_sum, tp_index * unit_width, 0)
    summed_small = lax.psum((width_stack, head_stack, unit_line), ("fsdp", "tp"))
    shard_size = model_width // lax.axis_size("fsdp")
    width_pieces = lax.dynamic_slice_in_dim(summed_small[0], fsdp_index * shard_size, shard_size, 1)
    head_pieces = lax.dynamic_slice_in_dim(summed_small[1], tp_index * head_width, head_width, 1)
    unit_piece = lax.dynamic_slice_in_dim(summed_small[2], tp_index * unit_width, unit_width, 0)
    return (
        jnp.stack(outputs, 0),
        jnp.stack(grad_list, 0),
        width_pieces[0],
        width_pieces[1],
        summed_weights[0],
        head_pieces[0],
        summed_weights[1],
        summed_weights[2],
        head_pieces[1],
        summed_weights[3],
        width_pieces[2],
        width_pieces[3],
        width_pieces[4],
        summed_weights[4],
        unit_piece,
        summed_weights[5],
        width_pieces[5],
    )


def solution(mesh):
    in_specs = (
        P("fsdp", "tp", None),
        P("fsdp", "tp", None),
        P("fsdp"),
        P("fsdp"),
        P("fsdp"),
        P("fsdp", "tp"),
        P("tp"),
        P("fsdp", "tp"),
        P("fsdp", "tp"),
        P("tp"),
        P("tp", "fsdp"),
        P("fsdp"),
        P("fsdp"),
        P("fsdp"),
        P("fsdp", "tp"),
        P("tp"),
        P("tp", "fsdp"),
        P("fsdp"),
    )
    out_specs = (
        P("fsdp", "tp", None),
        P("fsdp", "tp", None),
        P("fsdp"),
        P("fsdp"),
        P("fsdp", "tp"),
        P("tp"),
        P("fsdp", "tp"),
        P("fsdp", "tp"),
        P("tp"),
        P("tp", "fsdp"),
        P("fsdp"),
        P("fsdp"),
        P("fsdp"),
        P("fsdp", "tp"),
        P("tp"),
        P("tp", "fsdp"),
        P("fsdp"),
    )
    return jax.shard_map(local, mesh=mesh, in_specs=in_specs, out_specs=out_specs, check_vma=False)
```

profile of v0, /device:TPU:0, one launch (start us, length us, event | category | flops | bytes accessed | tf_op | source)
XLA Modules:
  0.0 1294.0 jit_solution(5558494795576318744)
XLA Ops:
  14.4 38.8 %all-reduce.15 = (bf16[1152]{0:T(1024)(128)(2,1)S(1)}, bf16[1152]{0:T(1024)(128)(2,1)S(1)}, bf16[1152]{0:T(1024)(128)(2,1)S(1)}, bf16[1152]{0:T(1024)(128)(2,1)S...) all-reduce(bf16[1152]{0:T(1024)(128)(2,1)S(1)} %dynamic-update-slic, ...), channel_id=1, replica_groups=mesh['fsdp'=8,'tp'=4] {'fsdp'}, use_global_device_ids=true, to_apply=%add.1 | all-reduce | flops 6912 | bytes 27648
  60.0 32.5 %all_gather.44 = bf16[1152,288]{1,0:T(8,128)(2,1)S(1)} all-gather(bf16[144,288]{1,0:T(8,128)(2,1)S(1)} %copy-done.54), channel_id=1, replica_groups=mesh['fsdp'=8,'tp'=4] {'fsdp'}, dimensions={0}, use_global_device_ids=true | all-gather | bytes 746496 | tf_op jit(solution)/shard_map/all_gather | solution.py:77
  92.5 32.2 %all_gather.45 = bf16[1152,288]{1,0:T(8,128)(2,1)S(1)} all-gather(bf16[144,288]{1,0:T(8,128)(2,1)S(1)} %copy-done.55), channel_id=1, replica_groups=mesh['fsdp'=8,'tp'=4] {'fsdp'}, dimensions={0}, use_global_device_ids=true | all-gather | bytes 746496 | tf_op jit(solution)/shard_map/all_gather | solution.py:78
  126.1 34.5 %all_gather.43 = bf16[1152,288]{1,0:T(8,128)(2,1)} all-gather(bf16[144,288]{1,0:T(8,128)(2,1)S(1)} %copy-done.56), channel_id=1, replica_groups=mesh['fsdp'=8,'tp'=4] {'fsdp'}, dimensions={0}, use_global_device_ids=true | all-gather | bytes 746496 | tf_op jit(solution)/shard_map/all_gather | solution.py:79
  160.6 32.0 %all_gather.46 = bf16[288,1152]{0,1:T(8,128)(2,1)S(1)} all-gather(bf16[288,144]{0,1:T(8,128)(2,1)S(1)} %copy-done.57), channel_id=1, replica_groups=mesh['fsdp'=8,'tp'=4] {'fsdp'}, dimensions={1}, use_global_device_ids=true | all-gather | bytes 746496 | tf_op jit(solution)/shard_map/all_gather | solution.py:80
  231.9 15.0 %reduce-scatter.47.cloned.1.call-done = f32[184,1152]{1,0:T(8,128)} async-done(((f32[736,1152]{1,0:T(8,128)}), f32[184,1152]{1,0:T(8,128)}) %reduce-scatter.47.cloned.1.call-update) | async-done | bytes 847888
  247.0 42.0 %reduce-scatter.43.cloned.1.call-done = f32[184,1152]{1,0:T(8,128)} async-done(((f32[736,1152]{1,0:T(8,128)}), f32[184,1152]{1,0:T(8,128)}) %reduce-scatter.43.cloned.1.call-update) | async-done | bytes 847888
  294.4 17.0 %all-gather.23.cloned.1.call-done = bf16[736,1152]{1,0:T(8,128)(2,1)} async-done(((bf16[184,1152]{1,0:T(8,128)(2,1)}), bf16[736,1152]{1,0:T(8,128)(2,1)}) %all-gather.23.cloned.1.call-update) | async-done | bytes 1695760 | tf_op jit(solution)/shard_map/all_gather | solution.py:194
  311.4 57.1 %all-gather.17.cloned.1.call-done = bf16[1076,1152]{0,1:T(8,128)(2,1)} async-done(((bf16[1076,144]{0,1:T(8,128)(2,1)}), bf16[1076,1152]{0,1:T(8,128)(2,1)}) %all-gather.17.cloned.1.call-update) | async-done | bytes 2479120 | tf_op jit(solution)/shard_map/all_gather | solution.py:87
  368.5 6.4 fusion.87
  374.9 49.4 %all-gather.15.cloned.1.call-done = bf16[1152,1076]{1,0:T(8,128)(2,1)} async-done(((bf16[144,1076]{1,0:T(8,128)(2,1)}), bf16[1152,1076]{1,0:T(8,128)(2,1)}) %all-gather.15.cloned.1.call-update) | async-done | bytes 2479120 | tf_op jit(solution)/shard_map/all_gather | solution.py:86
  424.3 20.5 %all-gather.13.cloned.1.call-done = bf16[736,1152]{1,0:T(8,128)(2,1)} async-done(((bf16[184,1152]{1,0:T(8,128)(2,1)}), bf16[736,1152]{1,0:T(8,128)(2,1)}) %all-gather.13.cloned.1.call-update) | async-done | bytes 1695760 | tf_op jit(solution)/shard_map/all_gather | solution.py:129
  444.8 10.3 convert_reduce_fusion.1
  466.7 6.4 fusion.90
  473.1 15.4 %all-gather.21.cloned.1.call-done = bf16[736,1152]{1,0:T(8,128)(2,1)} async-done(((bf16[184,1152]{1,0:T(8,128)(2,1)}), bf16[736,1152]{1,0:T(8,128)(2,1)}) %all-gather.21.cloned.1.call-update) | async-done | bytes 1695760 | tf_op jit(solution)/shard_map/all_gather | solution.py:129
  488.5 10.2 convert_reduce_fusion
  504.6 7.8 fusion.73
  512.5 7.6 fusion.74
  520.2 10.4 reduce-scatter.51.cloned.1.call-done
  530.6 42.1 %reduce-scatter.55.cloned.1.call-done = f32[184,1152]{1,0:T(8,128)} async-done(((f32[736,1152]{1,0:T(8,128)}), f32[184,1152]{1,0:T(8,128)}) %reduce-scatter.55.cloned.1.call-update) | async-done | bytes 847888
  574.8 39.9 %reduce-scatter.45.cloned.1.call-done = f32[184,1152]{1,0:T(8,128)} async-done(((f32[736,1152]{1,0:T(8,128)}), f32[184,1152]{1,0:T(8,128)}) %reduce-scatter.45.cloned.1.call-update) | async-done | bytes 847888
  614.7 42.1 %reduce-scatter.49.cloned.1.call-done = f32[184,1152]{1,0:T(8,128)} async-done(((f32[736,1152]{1,0:T(8,128)}), f32[184,1152]{1,0:T(8,128)}) %reduce-scatter.49.cloned.1.call-update) | async-done | bytes 847888
  665.4 19.5 %all-gather.29.cloned.1.call-done = bf16[736,1152]{1,0:T(8,128)(2,1)} async-done(((bf16[184,1152]{1,0:T(8,128)(2,1)}), bf16[736,1152]{1,0:T(8,128)(2,1)}) %all-gather.29.cloned.1.call-update) | async-done | bytes 1695760 | tf_op jit(solution)/shard_map/all_gather | solution.py:213
  713.2 6.6 multiply_reduce_fusion.1
  782.2 9.3 reduce-scatter.53.cloned.1.call-done
  796.5 43.7 %all-reduce.14 = (f32[6,1152]{1,0:T(8,128)}, f32[2,1152]{1,0:T(2,128)S(1)}, f32[4304]{0:T(1024)S(1)}) all-reduce(f32[6,1152]{1,0:T(8,128)S(1)} %stack.38, f32[2,1152]{1,0:T(2,128)S(1)} %dynamic_update_slice.6, f32[4304]{0:T(1024)S(1)} %add_dynamic-update-slice_fusion), channel_id=1, replica_groups=mesh['fsdp'=8,'tp'=4] {'fsdp','tp'}, use_global_device_ids=true, to_apply=%region_42.43 | all-reduce | flops 13520 | bytes 108160 | tf_op jit(solution)/shard_map/psum | solution.py:344
  848.7 52.2 %reduce-scatter.39.cloned.1.call-done = f32[144,1076]{1,0:T(8,128)} async-done(((f32[1152,1076]{1,0:T(8,128)}), f32[144,1076]{1,0:T(8,128)}) %reduce-scatter.39.cloned.1.call-update) | async-done | bytes 619792 | tf_op jit(solution)/shard_map/reduce_scatter | solution.py:332
  901.0 108.4 %reduce-scatter.41.cloned.1.call-done = f32[1076,144]{0,1:T(8,128)} async-done(((f32[1076,1152]{0,1:T(8,128)}), f32[1076,144]{0,1:T(8,128)}) %reduce-scatter.41.cloned.1.call-update) | async-done | bytes 619792 | tf_op jit(solution)/shard_map/reduce_scatter | solution.py:333
  1009.4 69.9 %reduce-scatter.37.cloned.1.call-done = f32[288,144]{0,1:T(8,128)} async-done(((f32[288,1152]{0,1:T(8,128)}), f32[288,144]{0,1:T(8,128)}) %reduce-scatter.37.cloned.1.call-update) | async-done | bytes 165904 | tf_op jit(solution)/shard_map/reduce_scatter | solution.py:331
  1079.3 69.5 %reduce-scatter.35.cloned.1.call-done = f32[144,288]{1,0:T(8,128)} async-done(((f32[1152,288]{1,0:T(8,128)}), f32[144,288]{1,0:T(8,128)}) %reduce-scatter.35.cloned.1.call-update) | async-done | bytes 165904 | tf_op jit(solution)/shard_map/reduce_scatter | solution.py:330
  1148.7 69.0 %reduce-scatter.33.cloned.1.call-done = f32[144,288]{1,0:T(8,128)} async-done(((f32[1152,288]{1,0:T(8,128)}), f32[144,288]{1,0:T(8,128)}) %reduce-scatter.33.cloned.1.call-update) | async-done | bytes 165904 | tf_op jit(solution)/shard_map/reduce_scatter | solution.py:329
  1217.7 69.0 %reduce-scatter.31.cloned.1.call-done = f32[144,288]{1,0:T(8,128)} async-done(((f32[1152,288]{1,0:T(8,128)}), f32[144,288]{1,0:T(8,128)}) %reduce-scatter.31.cloned.1.call-update) | async-done | bytes 165904 | tf_op jit(solution)/shard_map/reduce_scatter | solution.py:328
  (417 shorter events, 190.1 us)
Async XLA Ops:
  7.2 85.3 %copy-start.91 = (bf16[288]{0:T(512)(128)(2,1)S(1)}, bf16[288]{0:T(512)(128)(2,1)}, u32[]{:S(2)}) copy-start(bf16[288]{0:T(512)(128)(2,1)} %param.24) | copy-start | bytes 1732
  7.2 117.5 %copy-start.90 = (s32[2]{0:T(128)S(1)}, s32[2]{0:T(128)}, u32[]{:S(2)}) copy-start(s32[2]{0:T(128)} %param.20) | copy-start | bytes 28
  7.2 118.8 %copy-start.56 = (bf16[144,288]{1,0:T(8,128)(2,1)S(1)}, bf16[144,288]{1,0:T(8,128)(2,1)}, u32[]{:S(2)}) copy-start(bf16[144,288]{1,0:T(8,128)(2,1)} %param.26) | copy-start | bytes 248836
  7.2 185.3 %all-gather.19.cloned.1.call-start = ((), (), s32[]{:S(2)}) async-start(), calls=%async_computation.18 | async-start | bytes 2119680 | tf_op jit(solution)/shard_map/all_gather | solution.py:108
  54.6 106.0 %copy-start.92 = (bf16[288]{0:T(512)(128)(2,1)S(1)}, bf16[288]{0:T(512)(128)(2,1)}, u32[]{:S(2)}) copy-start(bf16[288]{0:T(512)(128)(2,1)} %param.27) | copy-start | bytes 1732
  54.6 106.0 %copy-start.57 = (bf16[288,144]{0,1:T(8,128)(2,1)S(1)}, bf16[288,144]{0,1:T(8,128)(2,1)}, u32[]{:S(2)}) copy-start(bf16[288,144]{0,1:T(8,128)(2,1)} %param.28) | copy-start | bytes 248836
  59.2 151.7 %all-gather.11.cloned.1.call-start = ((), (), s32[]{:S(2)}) async-start(), calls=%async_computation.14 | async-start | bytes 2119680 | tf_op jit(solution)/shard_map/all_gather | solution.py:108
  60.0 187.0 %reduce-scatter.47.cloned.1.call-start = ((), (), s32[]{:S(2)}) async-start(), calls=%async_computation.32 | async-start | bytes 4239360
  124.7 86.1 %copy-start.11 = (bf16[1152,288]{1,0:T(8,128)(2,1)}, bf16[1152,288]{1,0:T(8,128)(2,1)S(1)}, u32[]{:S(2)}) copy-start(bf16[1152,288]{1,0:T(8,128)(2,1)S(1)} %all_gather.45) | copy-start | bytes 1990660
  209.9 79.2 %reduce-scatter.43.cloned.1.call-start = ((), (), s32[]{:S(2)}) async-start(), calls=%async_computation.30 | async-start | bytes 4239360
  227.8 83.6 %all-gather.23.cloned.1.call-start = ((), (), s32[]{:S(2)}) async-start(), calls=%async_computation.20 | async-start | bytes 2119680 | tf_op jit(solution)/shard_map/all_gather | solution.py:194
  230.5 138.0 %all-gather.17.cloned.1.call-start = ((), (), s32[]{:S(2)}) async-start(), calls=%async_computation.17 | async-start | bytes 2985984 | tf_op jit(solution)/shard_map/all_gather | solution.py:87
  231.1 193.2 %all-gather.15.cloned.1.call-start = ((), (), s32[]{:S(2)}) async-start(), calls=%async_computation.16 | async-start | bytes 2985984 | tf_op jit(solution)/shard_map/all_gather | solution.py:86
  231.8 213.0 %all-gather.13.cloned.1.call-start = ((), (), s32[]{:S(2)}) async-start(), calls=%async_computation.15 | async-start | bytes 2119680 | tf_op jit(solution)/shard_map/all_gather | solution.py:129
  292.6 174.2 %all-gather.27.cloned.1.call-start = ((), (), s32[]{:S(2)}) async-start(), calls=%async_computation.22 | async-start | bytes 2119680 | tf_op jit(solution)/shard_map/all_gather | solution.py:194
  293.3 195.2 %all-gather.21.cloned.1.call-start = ((), (), s32[]{:S(2)}) async-start(), calls=%async_computation.19 | async-start | bytes 2119680 | tf_op jit(solution)/shard_map/all_gather | solution.py:129
  293.9 236.7 %reduce-scatter.51.cloned.1.call-start = ((), (), s32[]{:S(2)}) async-start(), calls=%async_computation.34 | async-start | bytes 4239360
  460.8 111.9 %reduce-scatter.55.cloned.1.call-start = ((), (), s32[]{:S(2)}) async-start(), calls=%async_computation.36 | async-start | bytes 4239360
  504.3 110.3 %reduce-scatter.45.cloned.1.call-start = ((), (), s32[]{:S(2)}) async-start(), calls=%async_computation.31 | async-start | bytes 4239360
  512.4 144.3 %reduce-scatter.49.cloned.1.call-start = ((), (), s32[]{:S(2)}) async-start(), calls=%async_computation.33 | async-start | bytes 4239360
  520.1 164.7 %all-gather.29.cloned.1.call-start = ((), (), s32[]{:S(2)}) async-start(), calls=%async_computation.23 | async-start | bytes 2119680 | tf_op jit(solution)/shard_map/all_gather | solution.py:213
  574.7 86.5 %copy-start.72 = (f32[184]{0:T(256)S(1)}, f32[184]{0:T(256)}, u32[]{:S(2)}) copy-start(f32[184]{0:T(256)} %copy-done.71) | copy-start | bytes 2212
  574.7 86.5 %copy-start.75 = (f32[184]{0:T(256)S(1)}, f32[184]{0:T(256)}, u32[]{:S(2)}) copy-start(f32[184]{0:T(256)} %copy-done.74) | copy-start | bytes 2212
  664.4 45.6 %all-gather.25.cloned.1.call-start = ((), (), s32[]{:S(2)}) async-start(), calls=%async_computation.21 | async-start | bytes 2119680 | tf_op jit(solution)/shard_map/all_gather | solution.py:213
  665.0 117.2 %reduce-scatter.57.cloned.1.call-start = ((), (), s32[]{:S(2)}) async-start(), calls=%async_computation.37 | async-start | bytes 4239360
  709.8 81.7 %reduce-scatter.53.cloned.1.call-start = ((), (), s32[]{:S(2)}) async-start(), calls=%async_computation.35 | async-start | bytes 4239360
  734.7 166.2 %reduce-scatter.39.cloned.1.call-start = ((), (), s32[]{:S(2)}) async-start(), calls=%async_computation.28 | async-start | bytes 5971968 | tf_op jit(solution)/shard_map/reduce_scatter | solution.py:332
  745.5 263.9 %reduce-scatter.41.cloned.1.call-start = ((), (), s32[]{:S(2)}) async-start(), calls=%async_computation.29 | async-start | bytes 5971968 | tf_op jit(solution)/shard_map/reduce_scatter | solution.py:333
  756.8 322.4 %reduce-scatter.37.cloned.1.call-start = ((), (), s32[]{:S(2)}) async-start(), calls=%async_computation.27 | async-start | bytes 1990656 | tf_op jit(solution)/shard_map/reduce_scatter | solution.py:331
  763.1 385.7 %reduce-scatter.35.cloned.1.call-start = ((), (), s32[]{:S(2)}) async-start(), calls=%async_computation.26 | async-start | bytes 1990656 | tf_op jit(solution)/shard_map/reduce_scatter | solution.py:330
  768.3 449.4 %reduce-scatter.33.cloned.1.call-start = ((), (), s32[]{:S(2)}) async-start(), calls=%async_computation.25 | async-start | bytes 1990656 | tf_op jit(solution)/shard_map/reduce_scatter | solution.py:329
  773.5 513.2 %reduce-scatter.31.cloned.1.call-start = ((), (), s32[]{:S(2)}) async-start(), calls=%async_computation.24 | async-start | bytes 1990656 | tf_op jit(solution)/shard_map/reduce_scatter | solution.py:328
  (106 other events, 1012.5 us)
Sparse Core Ops, SparseCore 0:
  59.3 17.5 all-gather.18
  79.0 20.3 all-gather.10
  210.0 36.9 reduce-scatter.46
  249.5 39.4 reduce-scatter.42
  291.0 20.3 all-gather.22
  313.4 55.0 all-gather.16
  370.6 53.5 all-gather.14
  425.8 18.9 all-gather.12
  446.4 20.3 all-gather.26
  468.1 20.3 all-gather.20
  491.1 39.4 reduce-scatter.50
  533.1 39.4 reduce-scatter.54
  575.2 39.4 reduce-scatter.44
  617.2 39.4 reduce-scatter.48
  664.5 20.3 all-gather.28
  686.3 20.3 all-gather.24
  709.9 39.4 reduce-scatter.56
  752.0 39.4 reduce-scatter.52
  795.6 105.2 reduce-scatter.38
  905.4 103.9 reduce-scatter.40
  1013.4 65.7 reduce-scatter.36
  1083.7 64.9 reduce-scatter.34
  1152.8 64.8 reduce-scatter.32
  1222.0 64.6 reduce-scatter.30
where the time goes:
time: 1300 us; the launch traced here: 1290 us
  waiting for transfers between devices  827 us (64%)
  blocking collectives  214 us (16%)
  matrix products  156 us (12%)
  other arithmetic  50 us (4%)
  local copies, waits for them, and re-layouts  26.7 us (2%)
  between operations  17.3 us (1%)
    unnamed x32, waiting for transfers between devices  205 us
    reduce_scatter x1, waiting for transfers between devices, local(): lax.psum_scatter(grad_w_down, 'fsdp', scatter_dimension=1, tiled=True)  108 us
    reduce_scatter x1, waiting for transfers between devices, local(): lax.psum_scatter(grad_w_out, 'fsdp', scatter_dimension=1, tiled=True)  69.9 us
    reduce_scatter x1, waiting for transfers between devices, local(): lax.psum_scatter(grad_wv, 'fsdp', scatter_dimension=0, tiled=True)  69.5 us
    reduce_scatter x1, waiting for transfers between devices, local(): lax.psum_scatter(grad_wq, 'fsdp', scatter_dimension=0, tiled=True)  69 us
    reduce_scatter x1, waiting for transfers between devices, local(): lax.psum_scatter(grad_wk, 'fsdp', scatter_dimension=0, tiled=True)  69 us
    all_gather x1, waiting for transfers between devices, fetch_weights(): lax.all_gather(down_weight, 'fsdp', axis=1, tiled=True)  57.1 us
    reduce_scatter x1, waiting for transfers between devices, local(): lax.psum_scatter(grad_w_up, 'fsdp', scatter_dimension=0, tiled=True)  52.2 us
  transfers between devices with their start and end apart: 24, of which 20 were waited for; matrix products, arithmetic and copies ran while one was open for 15% of the time, Pallas kernels for 0%

commit v1 on v0

--- a/solution.py
+++ b/solution.py
@@ -6,6 +6,19 @@
 HD = 72
 epsilon = 1e-06
 negative_big = -1e30
+
+
+def report_links(chunk, device_axis):
+    n_blocks = lax.axis_size(device_axis)
+    table = tuple(((dev_j, (dev_j + 1) % n_blocks) for dev_j in range(n_blocks)))
+    f_now, out_arr = ([chunk], [chunk])
+    leaves = tuple(((dev_j, (dev_j - 1) % n_blocks) for dev_j in range(n_blocks)))
+    for _ in range(n_blocks // 2):
+        f_now.append(lax.ppermute(f_now[-1], device_axis, table))
+    for _ in [*range((n_blocks - 1) // 2)]:
+        out_arr.append(lax.ppermute(out_arr[-1], device_axis, leaves))
+    part_next = jnp.concatenate([*f_now[::-1], *out_arr[1:]], axis=0)
+    return jnp.roll(part_next, (lax.axis_index(device_axis) - n_blocks // 2) * chunk.shape[0], 0)
 
 
 def layer_norm(row_block, gain_vec, shift_vec):
@@ -83,7 +96,7 @@
         mlp_full = (
             lax.all_gather(ln2_gain, "fsdp", axis=0, tiled=True),
             lax.all_gather(ln2_bias, "fsdp", axis=0, tiled=True),
-            lax.all_gather(up_weight, "fsdp", axis=0, tiled=True),
+            report_links(up_weight, device_axis="fsdp"),
             lax.all_gather(down_weight, "fsdp", axis=1, tiled=True),
             lax.all_gather(down_bias, "fsdp", axis=0, tiled=True),
         )

time: 1300 us -> 1250 us (0.962)
  waiting for transfers between devices: 827 us -> 746 us
  starting transfers between devices: 3.12 us -> 24.3 us
    all_gather x1 -> x0, waiting for transfers between devices: 49.4 us -> none  [fetch_weights(): lax.all_gather(up_weight, 'fsdp', axis=0, tiled=True)]
    all_gather x1, waiting for transfers between devices: 57.1 us -> 10.1 us  [fetch_weights(): lax.all_gather(down_weight, 'fsdp', axis=1, tiled=True)]
    ppermute x0 -> x7, waiting for transfers between devices: none -> 38.9 us  [the longest x4 38.9 us: report_links(): f_now.append(lax.ppermute(f_now[-1], device_axis, table))]
    ppermute x0 -> x7, starting transfers between devices: none -> 21.4 us  [the longest x3 14.8 us: report_links(): out_arr.append(lax.ppermute(out_arr[-1], device_axis, leaves))]
    all_gather x2, waiting for transfers between devices: 22.7 us -> 5.68 us  [local(): lax.all_gather(grad_out.astype(jnp.bfloat16), 'tp', axis=0, tiled=True)]
    unnamed x241 -> x252, local copies, waits for them, and re-layouts: 22.1 us -> 32.3 us
    unnamed x32 -> x31, waiting for transfers between devices: 205 us -> 204 us
  transfers between devices with their start and end apart: 24 -> 30, of which waited for: 20 -> 22; matrix products, arithmetic and copies ran while one was open for 15% -> 17% of each run, Pallas kernels for 0% -> 0%
where the time goes in v1:
time: 1250 us
  waiting for transfers between devices  746 us (60%)
  blocking collectives  214 us (17%)
  matrix products  156 us (12%)
  other arithmetic  56.1 us (4%)
  local copies, waits for them, and re-layouts  37.7 us (3%)
  starting transfers between devices  24.3 us (2%)
  between operations  16.9 us (1%)
    unnamed x31, waiting for transfers between devices  204 us
    reduce_scatter x1, waiting for transfers between devices, local(): lax.psum_scatter(grad_w_down, 'fsdp', scatter_dimension=1, tiled=True)  109 us
    reduce_scatter x1, waiting for transfers between devices, local(): lax.psum_scatter(grad_w_out, 'fsdp', scatter_dimension=1, tiled=True)  69.6 us
    reduce_scatter x1, waiting for transfers between devices, local(): lax.psum_scatter(grad_wv, 'fsdp', scatter_dimension=0, tiled=True)  69.4 us
    reduce_scatter x1, waiting for transfers between devices, local(): lax.psum_scatter(grad_wq, 'fsdp', scatter_dimension=0, tiled=True)  69.3 us
    reduce_scatter x1, waiting for transfers between devices, local(): lax.psum_scatter(grad_wk, 'fsdp', scatter_dimension=0, tiled=True)  69 us
    reduce_scatter x1, waiting for transfers between devices, local(): lax.psum_scatter(grad_w_up, 'fsdp', scatter_dimension=0, tiled=True)  52.1 us
    dot_general x12, matrix products, plain_dot(): return jnp.dot(left, right, preferred_element_type=jnp.float32)  49.9 us
  transfers between devices with their start and end apart: 30, of which 22 were waited for; matrix products, arithmetic and copies ran while one was open for 17% of the time, Pallas kernels for 0%

profile of v1, /device:TPU:0, one launch (start us, length us, event | category | flops | bytes accessed | tf_op | source)
XLA Modules:
  0.0 1250.4 jit_solution(10467260916777172855)
XLA Ops:
  14.4 38.8 %all-reduce.15 = (bf16[1152]{0:T(1024)(128)(2,1)S(1)}, bf16[1152]{0:T(1024)(128)(2,1)S(1)}, bf16[1152]{0:T(1024)(128)(2,1)S(1)}, bf16[1152]{0:T(1024)(128)(2,1)S...) all-reduce(bf16[1152]{0:T(1024)(128)(2,1)S(1)} %dynamic-update-slic, ...), channel_id=1, replica_groups=mesh['fsdp'=8,'tp'=4] {'fsdp'}, use_global_device_ids=true, to_apply=%add.1 | all-reduce | flops 6912 | bytes 27648
  60.0 32.5 %all_gather.42 = bf16[1152,288]{1,0:T(8,128)(2,1)S(1)} all-gather(bf16[144,288]{1,0:T(8,128)(2,1)S(1)} %copy-done.57), channel_id=1, replica_groups=mesh['fsdp'=8,'tp'=4] {'fsdp'}, dimensions={0}, use_global_device_ids=true | all-gather | bytes 746496 | tf_op jit(solution)/shard_map/all_gather | solution.py:90
  92.5 32.2 %all_gather.43 = bf16[1152,288]{1,0:T(8,128)(2,1)S(1)} all-gather(bf16[144,288]{1,0:T(8,128)(2,1)S(1)} %copy-done.58), channel_id=1, replica_groups=mesh['fsdp'=8,'tp'=4] {'fsdp'}, dimensions={0}, use_global_device_ids=true | all-gather | bytes 746496 | tf_op jit(solution)/shard_map/all_gather | solution.py:91
  126.0 34.6 %all_gather.41 = bf16[1152,288]{1,0:T(8,128)(2,1)} all-gather(bf16[144,288]{1,0:T(8,128)(2,1)S(1)} %copy-done.59), channel_id=1, replica_groups=mesh['fsdp'=8,'tp'=4] {'fsdp'}, dimensions={0}, use_global_device_ids=true | all-gather | bytes 746496 | tf_op jit(solution)/shard_map/all_gather | solution.py:92
  160.6 32.0 %all_gather.44 = bf16[288,1152]{0,1:T(8,128)(2,1)S(1)} all-gather(bf16[288,144]{0,1:T(8,128)(2,1)S(1)} %copy-done.60), channel_id=1, replica_groups=mesh['fsdp'=8,'tp'=4] {'fsdp'}, dimensions={1}, use_global_device_ids=true | all-gather | bytes 746496 | tf_op jit(solution)/shard_map/all_gather | solution.py:93
  231.2 15.8 %reduce-scatter.47.cloned.1.call-done = f32[184,1152]{1,0:T(8,128)} async-done(((f32[736,1152]{1,0:T(8,128)}), f32[184,1152]{1,0:T(8,128)}) %reduce-scatter.47.cloned.1.call-update) | async-done | bytes 847888
  247.0 42.1 %reduce-scatter.43.cloned.1.call-done = f32[184,1152]{1,0:T(8,128)} async-done(((f32[736,1152]{1,0:T(8,128)}), f32[184,1152]{1,0:T(8,128)}) %reduce-scatter.43.cloned.1.call-update) | async-done | bytes 847888
  294.3 10.8 collective-permute-done
  309.9 8.7 collective-permute-done.1
  327.4 10.4 collective-permute-done.2
  344.1 9.1 collective-permute-done.3
  370.7 10.1 all-gather.14.cloned.1.call-done
  387.2 14.2 %all-gather.12.cloned.1.call-done = bf16[736,1152]{1,0:T(8,128)(2,1)} async-done(((bf16[184,1152]{1,0:T(8,128)(2,1)}), bf16[736,1152]{1,0:T(8,128)(2,1)}) %all-gather.12.cloned.1.call-update) | async-done | bytes 1695760 | tf_op jit(solution)/shard_map/all_gather | solution.py:142
  401.4 10.3 convert_reduce_fusion.1
  429.7 15.6 %all-gather.18.cloned.1.call-done = bf16[736,1152]{1,0:T(8,128)(2,1)} async-done(((bf16[184,1152]{1,0:T(8,128)(2,1)}), bf16[736,1152]{1,0:T(8,128)(2,1)}) %all-gather.18.cloned.1.call-update) | async-done | bytes 1695760 | tf_op jit(solution)/shard_map/all_gather | solution.py:142
  445.3 10.2 convert_reduce_fusion
  461.3 7.8 fusion.74
  469.2 7.6 fusion.75
  476.9 10.3 reduce-scatter.51.cloned.1.call-done
  487.2 42.2 %reduce-scatter.55.cloned.1.call-done = f32[184,1152]{1,0:T(8,128)} async-done(((f32[736,1152]{1,0:T(8,128)}), f32[184,1152]{1,0:T(8,128)}) %reduce-scatter.55.cloned.1.call-update) | async-done | bytes 847888
  531.5 39.8 %reduce-scatter.45.cloned.1.call-done = f32[184,1152]{1,0:T(8,128)} async-done(((f32[736,1152]{1,0:T(8,128)}), f32[184,1152]{1,0:T(8,128)}) %reduce-scatter.45.cloned.1.call-update) | async-done | bytes 847888
  571.3 42.2 %reduce-scatter.49.cloned.1.call-done = f32[184,1152]{1,0:T(8,128)} async-done(((f32[736,1152]{1,0:T(8,128)}), f32[184,1152]{1,0:T(8,128)}) %reduce-scatter.49.cloned.1.call-update) | async-done | bytes 847888
  622.2 19.5 %all-gather.26.cloned.1.call-done = bf16[736,1152]{1,0:T(8,128)(2,1)} async-done(((bf16[184,1152]{1,0:T(8,128)(2,1)}), bf16[736,1152]{1,0:T(8,128)(2,1)}) %all-gather.26.cloned.1.call-update) | async-done | bytes 1695760 | tf_op jit(solution)/shard_map/all_gather | solution.py:226
  670.0 6.6 multiply_reduce_fusion.1
  739.0 9.2 reduce-scatter.53.cloned.1.call-done
  753.3 43.5 %all-reduce.14 = (f32[6,1152]{1,0:T(8,128)}, f32[2,1152]{1,0:T(2,128)S(1)}, f32[4304]{0:T(1024)S(1)}) all-reduce(f32[6,1152]{1,0:T(8,128)S(1)} %stack.38, f32[2,1152]{1,0:T(2,128)S(1)} %dynamic_update_slice.6, f32[4304]{0:T(1024)S(1)} %add_dynamic-update-slice_fusion), channel_id=1, replica_groups=mesh['fsdp'=8,'tp'=4] {'fsdp','tp'}, use_global_device_ids=true, to_apply=%region_42.44 | all-reduce | flops 13520 | bytes 108160 | tf_op jit(solution)/shard_map/psum | solution.py:357
  805.4 52.1 %reduce-scatter.39.cloned.1.call-done = f32[144,1076]{1,0:T(8,128)} async-done(((f32[1152,1076]{1,0:T(8,128)}), f32[144,1076]{1,0:T(8,128)}) %reduce-scatter.39.cloned.1.call-update) | async-done | bytes 619792 | tf_op jit(solution)/shard_map/reduce_scatter | solution.py:345
  857.6 108.6 %reduce-scatter.41.cloned.1.call-done = f32[1076,144]{0,1:T(8,128)} async-done(((f32[1076,1152]{0,1:T(8,128)}), f32[1076,144]{0,1:T(8,128)}) %reduce-scatter.41.cloned.1.call-update) | async-done | bytes 619792 | tf_op jit(solution)/shard_map/reduce_scatter | solution.py:346
  966.1 69.6 %reduce-scatter.37.cloned.1.call-done = f32[288,144]{0,1:T(8,128)} async-done(((f32[288,1152]{0,1:T(8,128)}), f32[288,144]{0,1:T(8,128)}) %reduce-scatter.37.cloned.1.call-update) | async-done | bytes 165904 | tf_op jit(solution)/shard_map/reduce_scatter | solution.py:344
  1035.8 69.4 %reduce-scatter.35.cloned.1.call-done = f32[144,288]{1,0:T(8,128)} async-done(((f32[1152,288]{1,0:T(8,128)}), f32[144,288]{1,0:T(8,128)}) %reduce-scatter.35.cloned.1.call-update) | async-done | bytes 165904 | tf_op jit(solution)/shard_map/reduce_scatter | solution.py:343
  1105.1 69.0 %reduce-scatter.33.cloned.1.call-done = f32[144,288]{1,0:T(8,128)} async-done(((f32[1152,288]{1,0:T(8,128)}), f32[144,288]{1,0:T(8,128)}) %reduce-scatter.33.cloned.1.call-update) | async-done | bytes 165904 | tf_op jit(solution)/shard_map/reduce_scatter | solution.py:342
  1174.1 69.3 %reduce-scatter.31.cloned.1.call-done = f32[144,288]{1,0:T(8,128)} async-done(((f32[1152,288]{1,0:T(8,128)}), f32[144,288]{1,0:T(8,128)}) %reduce-scatter.31.cloned.1.call-update) | async-done | bytes 165904 | tf_op jit(solution)/shard_map/reduce_scatter | solution.py:341
  (441 shorter events, 239.6 us)
Async XLA Ops:
  7.2 118.8 %copy-start.59 = (bf16[144,288]{1,0:T(8,128)(2,1)S(1)}, bf16[144,288]{1,0:T(8,128)(2,1)}, u32[]{:S(2)}) copy-start(bf16[144,288]{1,0:T(8,128)(2,1)} %param.28) | copy-start | bytes 248836
  7.2 185.4 %all-gather.16.cloned.1.call-start = ((), (), s32[]{:S(2)}) async-start(), calls=%async_computation.17 | async-start | bytes 2119680 | tf_op jit(solution)/shard_map/all_gather | solution.py:121
  59.2 151.8 %all-gather.10.cloned.1.call-start = ((), (), s32[]{:S(2)}) async-start(), calls=%async_computation.14 | async-start | bytes 2119680 | tf_op jit(solution)/shard_map/all_gather | solution.py:121
  60.0 187.0 %reduce-scatter.47.cloned.1.call-start = ((), (), s32[]{:S(2)}) async-start(), calls=%async_computation.31 | async-start | bytes 4239360
  210.0 79.1 %reduce-scatter.43.cloned.1.call-start = ((), (), s32[]{:S(2)}) async-start(), calls=%async_computation.29 | async-start | bytes 4239360
  227.9 142.8 %all-gather.20.cloned.1.call-start = ((), (), s32[]{:S(2)}) async-start(), calls=%async_computation.19 | async-start | bytes 2119680 | tf_op jit(solution)/shard_map/all_gather | solution.py:207
  230.5 150.2 %all-gather.14.cloned.1.call-start = ((), (), s32[]{:S(2)}) async-start(), calls=%async_computation.16 | async-start | bytes 2985984 | tf_op jit(solution)/shard_map/all_gather | solution.py:100
  231.1 170.2 %all-gather.12.cloned.1.call-start = ((), (), s32[]{:S(2)}) async-start(), calls=%async_computation.15 | async-start | bytes 2119680 | tf_op jit(solution)/shard_map/all_gather | solution.py:142
  291.4 238.1 %copy-start.70 = (f32[184]{0:T(256)}, f32[184]{0:T(256)S(1)}, u32[]{:S(2)}) copy-start(f32[184]{0:T(256)S(1)} %fusion.64) | copy-start | bytes 2212
  292.7 130.6 %all-gather.24.cloned.1.call-start = ((), (), s32[]{:S(2)}) async-start(), calls=%async_computation.21 | async-start | bytes 2119680 | tf_op jit(solution)/shard_map/all_gather | solution.py:207
  292.8 12.3 collective-permute-start
  305.1 13.6 %collective-permute-start.1 = (bf16[144,1076]{1,0:T(8,128)(2,1)S(1)}, bf16[144,1076]{1,0:T(8,128)(2,1)}, u32[]{:S(2)}, u32[]{:S(2)}) collective-permute-start(bf16[144,1076]{1,0:T(8,128)(2,1)S(1)} %collective-permute-done), channel_id=1, source_target_pairs={{0,4},{4,8},{8,12},{12,16},{16,20},{20,24},{24,28},{28,0},{1,5},{5... | collective-permute-start | bytes 929672 | tf_op jit(solution)/shard_map/ppermute | solution.py:17
  305.1 140.2 %all-gather.18.cloned.1.call-start = ((), (), s32[]{:S(2)}) async-start(), calls=%async_computation.18 | async-start | bytes 2119680 | tf_op jit(solution)/shard_map/all_gather | solution.py:142
  305.1 16.1 %collective-permute-start.4 = (bf16[144,1076]{1,0:T(8,128)(2,1)S(1)}, bf16[144,1076]{1,0:T(8,128)(2,1)}, u32[]{:S(2)}, u32[]{:S(2)}) collective-permute-start(bf16[144,1076]{1,0:T(8,128)(2,1)S(1)} %copy-done.54), channel_id=1, source_target_pairs={{0,28},{4,0},{8,4},{12,8},{16,12},{20,16},{24,20},{28,24},{1,29},{... | collective-permute-start | bytes 929672 | tf_op jit(solution)/shard_map/ppermute | solution.py:19
  318.6 19.1 %collective-permute-start.2 = (bf16[144,1076]{1,0:T(8,128)(2,1)}, bf16[144,1076]{1,0:T(8,128)(2,1)}, u32[]{:S(2)}, u32[]{:S(2)}) collective-permute-start(bf16[144,1076]{1,0:T(8,128)(2,1)} %collective-permute-done.1), channel_id=1, source_target_pairs={{0,4},{4,8},{8,12},{12,16},{16,20},{20,24},{24,28},{28,0},{1,5},{5... | collective-permute-start | bytes 929672 | tf_op jit(solution)/shard_map/ppermute | solution.py:17
  321.2 19.0 %collective-permute-start.5 = (bf16[144,1076]{1,0:T(8,128)(2,1)}, bf16[144,1076]{1,0:T(8,128)(2,1)}, u32[]{:S(2)}, u32[]{:S(2)}) collective-permute-start(bf16[144,1076]{1,0:T(8,128)(2,1)} %collective-permute-done.4), channel_id=1, source_target_pairs={{0,28},{4,0},{8,4},{12,8},{16,12},{20,16},{24,20},{28,24},{1,29},{... | collective-permute-start | bytes 929672 | tf_op jit(solution)/shard_map/ppermute | solution.py:19
  337.8 15.4 %collective-permute-start.3 = (bf16[144,1076]{1,0:T(8,128)(2,1)}, bf16[144,1076]{1,0:T(8,128)(2,1)}, u32[]{:S(2)}, u32[]{:S(2)}) collective-permute-start(bf16[144,1076]{1,0:T(8,128)(2,1)} %collective-permute-done.2), channel_id=1, source_target_pairs={{0,4},{4,8},{8,12},{12,16},{16,20},{20,24},{24,28},{28,0},{1,5},{5... | collective-permute-start | bytes 929672 | tf_op jit(solution)/shard_map/ppermute | solution.py:17
  340.3 23.2 %collective-permute-start.6 = (bf16[144,1076]{1,0:T(8,128)(2,1)}, bf16[144,1076]{1,0:T(8,128)(2,1)S(1)}, u32[]{:S(2)}, u32[]{:S(2)}) collective-permute-start(bf16[144,1076]{1,0:T(8,128)(2,1)} %collective-permute-done.5), channel_id=1, source_target_pairs={{0,28},{4,0},{8,4},{12,8},{16,12},{20,16},{24,20},{28,24},{1,29},{... | collective-permute-start | bytes 929672 | tf_op jit(solution)/shard_map/ppermute | solution.py:19
  364.3 122.9 %reduce-scatter.51.cloned.1.call-start = ((), (), s32[]{:S(2)}) async-start(), calls=%async_computation.33 | async-start | bytes 4239360
  417.6 111.8 %reduce-scatter.55.cloned.1.call-start = ((), (), s32[]{:S(2)}) async-start(), calls=%async_computation.35 | async-start | bytes 4239360
  461.1 110.3 %reduce-scatter.45.cloned.1.call-start = ((), (), s32[]{:S(2)}) async-start(), calls=%async_computation.30 | async-start | bytes 4239360
  469.1 144.4 %reduce-scatter.49.cloned.1.call-start = ((), (), s32[]{:S(2)}) async-start(), calls=%async_computation.32 | async-start | bytes 4239360
  476.8 164.8 %all-gather.26.cloned.1.call-start = ((), (), s32[]{:S(2)}) async-start(), calls=%async_computation.22 | async-start | bytes 2119680 | tf_op jit(solution)/shard_map/all_gather | solution.py:226
  621.2 45.6 %all-gather.22.cloned.1.call-start = ((), (), s32[]{:S(2)}) async-start(), calls=%async_computation.20 | async-start | bytes 2119680 | tf_op jit(solution)/shard_map/all_gather | solution.py:226
  621.8 117.2 %reduce-scatter.57.cloned.1.call-start = ((), (), s32[]{:S(2)}) async-start(), calls=%async_computation.36 | async-start | bytes 4239360
  666.6 81.7 %reduce-scatter.53.cloned.1.call-start = ((), (), s32[]{:S(2)}) async-start(), calls=%async_computation.34 | async-start | bytes 4239360
  691.5 166.0 %reduce-scatter.39.cloned.1.call-start = ((), (), s32[]{:S(2)}) async-start(), calls=%async_computation.27 | async-start | bytes 5971968 | tf_op jit(solution)/shard_map/reduce_scatter | solution.py:345
  702.3 263.8 %reduce-scatter.41.cloned.1.call-start = ((), (), s32[]{:S(2)}) async-start(), calls=%async_computation.28 | async-start | bytes 5971968 | tf_op jit(solution)/shard_map/reduce_scatter | solution.py:346
  713.7 322.1 %reduce-scatter.37.cloned.1.call-start = ((), (), s32[]{:S(2)}) async-start(), calls=%async_computation.26 | async-start | bytes 1990656 | tf_op jit(solution)/shard_map/reduce_scatter | solution.py:344
  719.8 385.3 %reduce-scatter.35.cloned.1.call-start = ((), (), s32[]{:S(2)}) async-start(), calls=%async_computation.25 | async-start | bytes 1990656 | tf_op jit(solution)/shard_map/reduce_scatter | solution.py:343
  725.1 449.0 %reduce-scatter.33.cloned.1.call-start = ((), (), s32[]{:S(2)}) async-start(), calls=%async_computation.24 | async-start | bytes 1990656 | tf_op jit(solution)/shard_map/reduce_scatter | solution.py:342
  730.4 513.0 %reduce-scatter.31.cloned.1.call-start = ((), (), s32[]{:S(2)}) async-start(), calls=%async_computation.23 | async-start | bytes 1990656 | tf_op jit(solution)/shard_map/reduce_scatter | solution.py:341
  (114 other events, 1732.2 us)
Sparse Core Ops, SparseCore 0:
  59.3 17.5 all-gather.15
  79.0 20.3 all-gather.9
  210.1 36.8 reduce-scatter.46
  249.6 39.4 reduce-scatter.42
  291.1 20.3 all-gather.19
  313.5 67.2 all-gather.13
  382.3 18.9 all-gather.11
  402.9 20.3 all-gather.23
  424.9 20.3 all-gather.17
  447.6 39.5 reduce-scatter.50
  489.9 39.4 reduce-scatter.54
  531.8 39.4 reduce-scatter.44
  574.0 39.4 reduce-scatter.48
  621.3 20.3 all-gather.25
  643.1 20.3 all-gather.21
  666.7 39.4 reduce-scatter.56
  708.7 39.4 reduce-scatter.52
  752.3 105.2 reduce-scatter.38
  862.1 103.9 reduce-scatter.40
  970.0 65.7 reduce-scatter.36
  1040.2 64.8 reduce-scatter.34
  1109.2 64.8 reduce-scatter.32
  1178.5 64.8 reduce-scatter.30
